TPU v7x, 32 devices: a whole 2x2x4 slice. The times are simulated.
32 devices in a mesh: expert: 16 (over z, y, x), tok: 2 (over core).
Axes of the slice: x: 2, y: 2, z: 4, core: 2. Of those that a mesh axis runs over, the one named last changes fastest.
Arguments:
- tokens: bfloat16 [2048, 3584], P(('expert', 'tok')), may hold values from -6 to 6
- routes: int32 [2048, 8], P(('expert', 'tok')), may hold values from 0 to 15, all different within a row; in each aligned block of 64 rows (0 to 63, 64 to 127, ...) at most 36 rows name the same one
- gates: float32 [2048, 8], P(('expert', 'tok')), may hold values from 0.05 to 1
- upstream: bfloat16 [2048, 3584], P(('expert', 'tok')), may hold values from -6 to 6
- w_up: bfloat16 [16, 3584, 1024], P('expert', None, 'tok'), may hold values from -0.09375 to 0.09375
- w_down: bfloat16 [16, 1024, 3584], P('expert', 'tok'), may hold values from -0.1875 to 0.1875
Outputs:
- mixed: bfloat16 [2048, 3584], P(('expert', 'tok'))
- d_tokens: bfloat16 [2048, 3584], P(('expert', 'tok'))
- d_gates: float32 [2048, 8], P(('expert', 'tok'))
- grad_up: bfloat16 [16, 3584, 1024], P('expert', None, 'tok')
- grad_down: bfloat16 [16, 1024, 3584], P('expert', 'tok')
Inputs may be any that keep to these rules, and one draw needn't show every extreme that they name: `routes`: each token names 8 different experts. At most 36 of the 64 tokens of one device name the same expert, and in every draw the tokens of some device name some expert exactly 36 times.
All inputs are finite; a program needn't handle non-finite values.
Results may differ from a plain program's by a relative error of at most 0.0065.
Values may be sent and summed in bfloat16 or wider, within the bound.
A program may use at most 192 MiB of HBM per device.

v0:
```python
import jax
import jax.numpy as jnp
from jax import lax
from jax.sharding import PartitionSpec as P

GELU_C = 0.7978845608028654
GELU_A = 0.044715


def gelu_value(hidden):
    inner_arg = GELU_C * (hidden + GELU_A * hidden * hidden * hidden)
    return 0.5 * hidden * (1.0 + jnp.tanh(inner_arg))


def gelu_slope(hidden):
    tangent = jnp.tanh(GELU_C * (hidden + GELU_A * hidden * hidden * hidden))
    return 0.5 * (1.0 + tangent) + 0.5 * hidden * (1.0 - tangent * tangent) * GELU_C * (
        1.0 + 3.0 * GELU_A * hidden * hidden
    )


def expert_rows(rows_x, rows_grad, up_local, down_local):
    hidden = jnp.dot(rows_x, up_local, preferred_element_type=jnp.float32)
    active = gelu_value(hidden).astype(jnp.bfloat16)
    out_part = jnp.dot(active, down_local, preferred_element_type=jnp.float32)
    d_active = lax.dot_general(
        rows_grad, down_local, (((1,), (1,)), ((), ())), preferred_element_type=jnp.float32
    )
    d_hidden = (d_active * gelu_slope(hidden)).astype(jnp.bfloat16)
    dx_part = lax.dot_general(
        d_hidden, up_local, (((1,), (1,)), ((), ())), preferred_element_type=jnp.float32
    )
    grad_down = lax.dot_general(
        active, rows_grad, (((0,), (0,)), ((), ())), preferred_element_type=jnp.float32
    )
    grad_up = lax.dot_general(
        rows_x, d_hidden, (((0,), (0,)), ((), ())), preferred_element_type=jnp.float32
    )
    return (out_part, dx_part, grad_up, grad_down)


def routed_shards(tokens, routes, gates, upstream, w_up, w_down):
    tok_rows, feature_width = tokens.shape
    top_count = routes.shape[1]
    owners = lax.axis_size("expert")
    pair_count = lax.axis_size("tok")
    capacity = tok_rows * top_count // owners + max(1, tok_rows * top_count // (8 * owners))
    assigned = routes.reshape(-1)
    labels = jnp.arange(owners, dtype=jnp.int32)
    onehot = (assigned[:, None] == labels[None, :]).astype(jnp.int32)
    earlier = jnp.cumsum(onehot, axis=0) - onehot
    slot_rank = jnp.sum(earlier * onehot, axis=1)
    slot_of = assigned * capacity + slot_rank
    slot_ids = jnp.arange(owners * capacity, dtype=jnp.int32)
    matches = (slot_of[None, :] == slot_ids[:, None]).astype(jnp.int32)
    filled = jnp.sum(matches, axis=1) > 0
    source = jnp.sum(matches * jnp.arange(assigned.shape[0], dtype=jnp.int32)[None, :], axis=1)
    token_ids = source // top_count
    send_x = jnp.where(filled[:, None], tokens[token_ids], jnp.zeros((), jnp.bfloat16))
    gate_rows = jnp.where(filled, gates.reshape(-1)[source], jnp.zeros((), jnp.float32))
    send_grad = (gate_rows[:, None] * upstream[token_ids].astype(jnp.float32)).astype(jnp.bfloat16)
    send_x = send_x.reshape(owners, capacity, feature_width)
    send_grad = send_grad.reshape(owners, capacity, feature_width)
    recv_x, recv_grad = (
        lax.all_to_all(send_x, "expert", split_axis=0, concat_axis=0, tiled=True),
        lax.all_to_all(send_grad, "expert", split_axis=0, concat_axis=0, tiled=True),
    )
    both_x, both_grad = (
        lax.all_gather(recv_x[None], "tok", axis=0, tiled=True),
        lax.all_gather(recv_grad[None], "tok", axis=0, tiled=True),
    )
    rows_x = both_x.reshape(-1, feature_width)
    rows_grad = both_grad.reshape(-1, feature_width)
    out_part, dx_part, grad_up, grad_down = expert_rows(rows_x, rows_grad, w_up[0], w_down[0])
    shaped_out = out_part.reshape(pair_count, owners, capacity, feature_width)
    shaped_dx = dx_part.reshape(pair_count, owners, capacity, feature_width)
    summed_out, summed_dx = (
        lax.psum_scatter(shaped_out, "tok", scatter_dimension=0, tiled=True),
        lax.psum_scatter(shaped_dx, "tok", scatter_dimension=0, tiled=True),
    )
    home_out, home_dx = (
        lax.all_to_all(
            summed_out[0].astype(jnp.bfloat16), "expert", split_axis=0, concat_axis=0, tiled=True
        ),
        lax.all_to_all(
            summed_dx[0].astype(jnp.bfloat16), "expert", split_axis=0, concat_axis=0, tiled=True
        ),
    )
    out_pairs = (
        home_out.reshape(owners * capacity, feature_width)[slot_of]
        .reshape(tok_rows, top_count, feature_width)
        .astype(jnp.float32)
    )
    dx_pairs = (
        home_dx.reshape(owners * capacity, feature_width)[slot_of]
        .reshape(tok_rows, top_count, feature_width)
        .astype(jnp.float32)
    )
    mixed_out = jnp.sum(gates[:, :, None] * out_pairs, axis=1).astype(jnp.bfloat16)
    d_gates = jnp.sum(upstream.astype(jnp.float32)[:, None, :] * out_pairs, axis=2)
    d_tokens = jnp.sum(dx_pairs, axis=1).astype(jnp.bfloat16)
    return (
        mixed_out,
        d_tokens,
        d_gates,
        grad_up.astype(jnp.bfloat16)[None],
        grad_down.astype(jnp.bfloat16)[None],
    )


def swapped(array, bit):
    return lax.ppermute(array, "expert", tuple(((i, i ^ bit) for i in range(16))))


def shifted(array, step, senders):
    return lax.ppermute(
        array,
        "expert",
        tuple(((i, i + 4 * step) for z in senders for i in range(4 * z, 4 * z + 4))),
    )


def add_rows(first, *others):
    total = first.astype(jnp.float32)
    for other in others:
        total = total + other.astype(jnp.float32)
    return total.astype(jnp.bfloat16)


def gathered_slots(block, layer, first, second):
    up_one = shifted(block, 1, (0, 1, 2))
    down_one = shifted(block, -1, (3, 2, 1))
    up_two = shifted(up_one, 1, (1, 2))
    down_two = shifted(down_one, -1, (2, 1))
    up_three = shifted(up_two, 1, (2,))
    down_three = shifted(down_two, -1, (1,))
    low = layer < 2
    far = jnp.where(
        low, jnp.where(layer == 0, down_three, up_one), jnp.where(layer == 3, up_three, down_one)
    )
    columns = (block, jnp.where(low, down_one, up_one), jnp.where(low, down_two, up_two), far)
    slots = []
    for column in columns:
        pair = jnp.stack([column, swapped(column, first)])
        other = swapped(pair, second)
        if first == 1:
            slots.append(jnp.concatenate([pair[0], pair[1], other[0], other[1]], axis=0))
        else:
            slots.append(jnp.concatenate([pair[0], other[0], pair[1], other[1]], axis=0))
    return slots


def scattered_column(rows, tok_rows, first, second):
    blocks = [rows[i * tok_rows : (i + 1) * tok_rows].astype(jnp.bfloat16) for i in range(4)]
    kept, sent = ((0, 1), (2, 3)) if first == 2 else ((0, 2), (1, 3))
    came = swapped(jnp.stack([blocks[i] for i in sent]), first)
    near = add_rows(blocks[kept[0]], came[0])
    far = add_rows(blocks[kept[1]], came[1])
    return add_rows(near, swapped(far, second))


def scattered_layers(columns, layer):
    up = shifted(columns[3], 1, (0,))
    down = shifted(columns[3], -1, (3,))
    up = shifted(add_rows(columns[2], up), 1, (0, 1))
    down = shifted(add_rows(columns[2], down), -1, (3, 2))
    up = shifted(add_rows(jnp.where(layer == 2, columns[3], columns[1]), up), 1, (0, 1, 2))
    down = shifted(add_rows(jnp.where(layer == 1, columns[3], columns[1]), down), -1, (3, 2, 1))
    return add_rows(columns[0], up, down)


def transposed_dot(rows, weights):
    return lax.dot_general(
        rows, weights, (((1,), (1,)), ((), ())), preferred_element_type=jnp.float32
    )


def outer(rows, columns):
    return lax.dot_general(
        rows, columns, (((0,), (0,)), ((), ())), preferred_element_type=jnp.float32
    )


def dense_shards(tokens, routes, gates, upstream, w_up, w_down):
    tok_rows, width = tokens.shape
    owners = lax.axis_size("expert")
    half = w_up.shape[2]
    swap = ((0, 1), (1, 0))
    mine = lax.axis_index("expert")
    layer = mine // 4
    up_local, down_local = (w_up[0], w_down[0])
    named = routes[:, :, None] == jnp.arange(owners, dtype=jnp.int32)
    gate_of = jnp.sum(jnp.where(named, gates[:, :, None], 0.0), axis=1)
    gate_all = lax.all_gather(gate_of, "expert", axis=0, tiled=True).reshape(
        owners, tok_rows, owners
    )
    gate_mine = lax.dynamic_index_in_dim(gate_all, mine, axis=2, keepdims=False)
    layers = (
        layer,
        jnp.where(layer < 2, layer + 1, layer - 1),
        jnp.where(layer < 2, layer + 2, layer - 2),
        jnp.where(layer % 2 == 0, 3, 0),
    )
    sources = [jnp.stack([z * 4 + (mine % 4 ^ flip) for flip in range(4)]) for z in layers]
    slots_x = gathered_slots(tokens, layer, 1, 2)
    slots_u = gathered_slots(upstream, layer, 2, 1)
    up_full = jnp.concatenate([up_local, lax.ppermute(up_local, "tok", swap)], axis=1)
    down_full = jnp.concatenate([down_local, lax.ppermute(down_local, "tok", swap)], axis=0)
    gated, slopes, inners = ([None] * 4, [None] * 4, [None] * 4)
    mixed_columns, dx_columns = ([None] * 4, [None] * 4)
    for s in range(4):
        gate = gate_mine[sources[s]].reshape(-1)[:, None]
        hidden = jnp.dot(slots_x[s], up_full, preferred_element_type=jnp.float32)
        value = gelu_value(hidden)
        gated[s] = (gate * value).astype(jnp.bfloat16)
        back = transposed_dot(slots_u[s], down_full)
        inners[s] = jnp.sum(value * back, axis=1).reshape(4, tok_rows)
        slopes[s] = (gate * back * gelu_slope(hidden)).astype(jnp.bfloat16)
    for s in (3, 2, 1, 0):
        out_part = jnp.dot(gated[s], down_full, preferred_element_type=jnp.float32)
        mixed_columns[s] = scattered_column(out_part, tok_rows, 2, 1)
        dx_part = transposed_dot(slopes[s], up_full)
        dx_columns[s] = scattered_column(dx_part, tok_rows, 1, 2)
    mixed = scattered_layers(mixed_columns, layer)
    d_tokens = scattered_layers(dx_columns, layer)
    order = jnp.concatenate(sources)
    inner = jnp.zeros((owners, tok_rows), jnp.float32).at[order].set(jnp.concatenate(inners))
    inner_all = lax.all_gather(inner, "expert", axis=0, tiled=True).reshape(
        owners, owners, tok_rows
    )
    home = lax.dynamic_index_in_dim(inner_all, mine, axis=1, keepdims=False)
    d_gates = jnp.sum(jnp.where(named, home.T[:, None, :], 0.0), axis=2)
    all_x, all_u = (jnp.concatenate(slots_x), jnp.concatenate(slots_u))
    act, d_hidden = (jnp.concatenate(gated), jnp.concatenate(slopes))
    down_far = outer(act[:, half:], all_u).astype(jnp.bfloat16)
    up_far = outer(all_x, d_hidden[:, half:]).astype(jnp.bfloat16)
    down_near = outer(act[:, :half], all_u)
    up_near = outer(all_x, d_hidden[:, :half])
    grad_down = down_near + lax.ppermute(down_far, "tok", swap).astype(jnp.float32)
    grad_up = up_near + lax.ppermute(up_far, "tok", swap).astype(jnp.float32)
    return (
        mixed,
        d_tokens,
        d_gates,
        grad_up.astype(jnp.bfloat16)[None],
        grad_down.astype(jnp.bfloat16)[None],
    )


def shards(tokens, routes, gates, upstream, w_up, w_down):
    dense = lax.axis_size("expert") == 16 and lax.axis_size("tok") == 2
    body = dense_shards if dense else routed_shards
    return body(tokens, routes, gates, upstream, w_up, w_down)


def solution(mesh):
    return jax.shard_map(
        shards,
        mesh=mesh,
        in_specs=(
            P(("expert", "tok"), None),
            P(("expert", "tok"), None),
            P(("expert", "tok"), None),
            P(("expert", "tok"), None),
            P("expert", None, "tok"),
            P("expert", "tok", None),
        ),
        out_specs=(
            P(("expert", "tok"), None),
            P(("expert", "tok"), None),
            P(("expert", "tok"), None),
            P("expert", None, "tok"),
            P("expert", "tok", None),
        ),
        check_vma=False,
    )
```

profile of v0, /device:TPU:20, one launch (start us, length us, event | category | flops | bytes accessed | tf_op | source)
XLA Modules:
  0.0 542.9 jit_solution(3025906620837556485)
XLA Ops:
  18.8 5.5 %collective-permute-done.30 = bf16[64,3584]{1,0:T(8,128)(2,1)S(1)} collective-permute-done((bf16[64,3584]{1,0:T(8,128)(2,1)}, bf16[64,3584]{1,0:T(8,128)(2,1)S(1)}, u32[]{:S(2)}, u32[]{:S(2)}) %collective-permute-start.30) | collective-permute-done | bytes 458784 | tf_op jit(solution)/shard_map/ppermute | solution.py:112
  27.9 13.7 %collective-permute-done.1 = bf16[2,64,3584]{2,1,0:T(8,128)(2,1)S(1)} collective-permute-done((bf16[2,64,3584]{2,1,0:T(8,128)(2,1)S(1)}, bf16[2,64,3584]{2,1,0:T(8,128)(2,1)S(1)}, u32[]{:S(2)}, u32[]{:S(2)}) %collective-permute-start.1) | collective-permute-done | bytes 917536 | tf_op jit(solution)/shard_map/ppermute | solution.py:112
  43.8 17.9 %collective-permute-done.31 = bf16[2,64,3584]{2,1,0:T(8,128)(2,1)S(1)} collective-permute-done((bf16[2,64,3584]{2,1,0:T(8,128)(2,1)S(1)}, bf16[2,64,3584]{2,1,0:T(8,128)(2,1)S(1)}, u32[]{:S(2)}, u32[]{:S(2)}) %collective-permute-start.31) | collective-permute-done | bytes 917536 | tf_op jit(solution)/shard_map/ppermute | solution.py:112
  71.0 9.9 %collective-permute-done.16 = bf16[64,3584]{1,0:T(8,128)(2,1)S(1)} collective-permute-done((bf16[64,3584]{1,0:T(8,128)(2,1)S(1)}, bf16[64,3584]{1,0:T(8,128)(2,1)S(1)}, u32[]{:S(2)}, u32[]{:S(2)}) %collective-permute-start.16) | collective-permute-done | bytes 458784 | tf_op jit(solution)/shard_map/ppermute | solution.py:112
  84.6 17.6 %collective-permute-done.17 = bf16[2,64,3584]{2,1,0:T(8,128)(2,1)S(1)} collective-permute-done((bf16[2,64,3584]{2,1,0:T(8,128)(2,1)S(1)}, bf16[2,64,3584]{2,1,0:T(8,128)(2,1)S(1)}, u32[]{:S(2)}, u32[]{:S(2)}) %collective-permute-start.17) | collective-permute-done | bytes 917536 | tf_op jit(solution)/shard_map/ppermute | solution.py:112
  104.9 17.5 %collective-permute-done.45 = bf16[2,64,3584]{2,1,0:T(8,128)(2,1)S(1)} collective-permute-done((bf16[2,64,3584]{2,1,0:T(8,128)(2,1)S(1)}, bf16[2,64,3584]{2,1,0:T(8,128)(2,1)S(1)}, u32[]{:S(2)}, u32[]{:S(2)}) %collective-permute-start.45) | collective-permute-done | bytes 917536 | tf_op jit(solution)/shard_map/ppermute | solution.py:112
  135.2 4.6 collective-permute-done.38
  143.7 4.6 collective-permute-done.20
  150.6 6.1 %collective-permute-done.48 = bf16[64,3584]{1,0:T(8,128)(2,1)S(1)} collective-permute-done((bf16[64,3584]{1,0:T(8,128)(2,1)S(1)}, bf16[64,3584]{1,0:T(8,128)(2,1)S(1)}, u32[]{:S(2)}, u32[]{:S(2)}) %collective-permute-start.48) | collective-permute-done | bytes 458784 | tf_op jit(solution)/shard_map/ppermute | solution.py:112
  159.2 5.4 collective-permute-start.39
  173.6 6.8 %multiply_reduce_fusion.2 = (f32[256]{0:T(256)S(1)}, f32[256,1024]{1,0:T(8,128)}) fusion(f32[256,1024]{1,0:T(8,128)} %fusion.18, bf16[512,3584]{1,0:T(8,128)(2,1)} %copy-done.39, bf16[512,3584]{1,0:T(8,128)(2,1)} %bitcast.290, bf16[64,3584]{1,0:T(8,128)(2,1)} %get-tuple-element.58, bf16[64,3584]{1,0:T(8,128)(2,1)S(1)} %collective-permute-done.44, ...), kind=kOutput, calls=%fused_computation.133 | convolution fusion | flops 1903689472 | bytes 11273216 | tf_op jit(solution)/shard_map/dot_general | solution.py:173
  186.5 11.9 %collective-permute-done.49 = bf16[2,64,3584]{2,1,0:T(8,128)(2,1)S(1)} collective-permute-done((bf16[2,64,3584]{2,1,0:T(8,128)(2,1)}, bf16[2,64,3584]{2,1,0:T(8,128)(2,1)S(1)}, u32[]{:S(2)}, u32[]{:S(2)}) %collective-permute-start.49) | collective-permute-done | bytes 917536 | tf_op jit(solution)/shard_map/ppermute | solution.py:112
  211.7 5.0 collective-permute-done.40
  220.1 6.6 %collective-permute-done.13 = bf16[2,64,3584]{2,1,0:T(8,128)(2,1)S(1)} collective-permute-done((bf16[2,64,3584]{2,1,0:T(8,128)(2,1)S(1)}, bf16[2,64,3584]{2,1,0:T(8,128)(2,1)S(1)}, u32[]{:S(2)}, u32[]{:S(2)}) %collective-permute-start.13) | collective-permute-done | bytes 917536 | tf_op jit(solution)/shard_map/ppermute | solution.py:112
  238.4 33.8 %all_gather.7 = f32[256,64]{1,0:T(8,128)S(1)} all-gather(f32[16,64]{1,0:T(8,128)S(1)} %scatter_custom_fusion), channel_id=1, replica_groups=mesh['expert'=16,'tok'=2] {'expert'}, dimensions={0}, use_global_device_ids=true | all-gather | bytes 69632 | tf_op jit(solution)/shard_map/all_gather | solution.py:228
  272.8 33.2 %all-gather = f32[16,64,16]{1,2,0:T(8,128)S(1)} all-gather(f32[1,64,16]{1,2,0:T(8,128)S(1)} %bitcast.279), channel_id=1, replica_groups=mesh['expert'=16,'tok'=2] {'expert'}, dimensions={0}, use_global_device_ids=true | all-gather | bytes 69632 | tf_op jit(solution)/shard_map/all_gather | solution.py:194
  310.9 5.3 convolution_convert_fusion.5
  328.6 5.3 convolution_convert_fusion.4
  334.0 5.3 convolution_convert_fusion.2
  341.7 4.3 convolution_convert_fusion.9
  350.6 5.2 convolution_convert_fusion.8
  355.9 5.2 convolution_convert_fusion.6
  364.1 8.6 %convolution_convert_fusion = bf16[512,3584]{1,0:T(8,128)(2,1)} fusion(bf16[1024,3584]{1,0:T(8,128)(2,1)} %constant_dynamic-update-slice_fusion.16, bf16[1024,1024]{1,0:T(8,128)(2,1)S(1)} %pad_maximum_fusion.3), kind=kOutput, calls=%fused_computation.9 | convolution fusion | flops 3759931392 | bytes 12058624 | tf_op jit(solution)/shard_map/dot_general | solution.py:179
  374.2 8.6 %convolution_convert_fusion.1 = bf16[3584,512]{1,0:T(8,128)(2,1)} fusion(bf16[1024,3584]{1,0:T(8,128)(2,1)} %constant_dynamic-update-slice_fusion, bf16[1024,1024]{1,0:T(8,128)(2,1)S(1)} %pad_maximum_fusion.2), kind=kOutput, calls=%fused_computation.10 | convolution fusion | flops 3759931392 | bytes 12058624 | tf_op jit(solution)/shard_map/dot_general | solution.py:179
  392.3 10.4 %collective-permute-done.18 = bf16[2,64,3584]{2,1,0:T(8,128)(2,1)S(1)} collective-permute-done((bf16[2,64,3584]{2,1,0:T(8,128)(2,1)S(1)}, bf16[2,64,3584]{2,1,0:T(8,128)(2,1)S(1)}, u32[]{:S(2)}, u32[]{:S(2)}) %collective-permute-start.18) | collective-permute-done | bytes 917536 | tf_op jit(solution)/shard_map/ppermute | solution.py:112
  402.9 25.5 %collective-permute-done.14 = bf16[2,64,3584]{2,1,0:T(8,128)(2,1)S(1)} collective-permute-done((bf16[2,64,3584]{2,1,0:T(8,128)(2,1)S(1)}, bf16[2,64,3584]{2,1,0:T(8,128)(2,1)S(1)}, u32[]{:S(2)}, u32[]{:S(2)}) %collective-permute-start.14) | collective-permute-done | bytes 917536 | tf_op jit(solution)/shard_map/ppermute | solution.py:112
  429.2 12.3 %collective-permute-done.43 = bf16[64,3584]{1,0:T(8,128)(2,1)S(1)} collective-permute-done((bf16[64,3584]{1,0:T(8,128)(2,1)S(1)}, bf16[64,3584]{1,0:T(8,128)(2,1)S(1)}, u32[]{:S(2)}, u32[]{:S(2)}) %collective-permute-start.43) | collective-permute-done | bytes 458784 | tf_op jit(solution)/shard_map/ppermute | solution.py:112
  445.5 17.4 %collective-permute-done.55 = bf16[64,3584]{1,0:T(8,128)(2,1)S(1)} collective-permute-done((bf16[64,3584]{1,0:T(8,128)(2,1)S(1)}, bf16[64,3584]{1,0:T(8,128)(2,1)S(1)}, u32[]{:S(2)}, u32[]{:S(2)}) %collective-permute-start.55) | collective-permute-done | bytes 458784 | tf_op jit(solution)/shard_map/ppermute | solution.py:116
  465.3 12.5 %collective-permute-done.27 = bf16[64,3584]{1,0:T(8,128)(2,1)S(1)} collective-permute-done((bf16[64,3584]{1,0:T(8,128)(2,1)S(1)}, bf16[64,3584]{1,0:T(8,128)(2,1)S(1)}, u32[]{:S(2)}, u32[]{:S(2)}) %collective-permute-start.27) | collective-permute-done | bytes 458784 | tf_op jit(solution)/shard_map/ppermute | solution.py:116
  479.1 4.6 collective-permute-start.56
  525.1 8.9 %fusion = bf16[1,3584,512]{2,1,0:T(8,128)(2,1)} fusion(bf16[3584,512]{1,0:T(8,128)(2,1)S(1)} %collective-permute-done.58, bf16[1024,3584]{1,0:T(8,128)(2,1)} %constant_dynamic-update-slice_fusion, bf16[1024,1024]{1,0:T(8,128)(2,1)S(1)} %pad_maximum_fusion.2), kind=kOutput, calls=%fused_computation.11 | convolution fusion | flops 3763601408 | bytes 15728640 | tf_op jit(solution)/shard_map/dot_general | solution.py:179
  534.0 8.7 %fusion.1 = bf16[1,512,3584]{2,1,0:T(8,128)(2,1)} fusion(bf16[512,3584]{1,0:T(8,128)(2,1)S(1)} %collective-permute-done.59, bf16[1024,3584]{1,0:T(8,128)(2,1)} %constant_dynamic-update-slice_fusion.16, bf16[1024,1024]{1,0:T(8,128)(2,1)S(1)} %pad_maximum_fusion.3), kind=kOutput, calls=%fused_computation.12 | convolution fusion | flops 3763601408 | bytes 15728640 | tf_op jit(solution)/shard_map/dot_general | solution.py:179
  (312 shorter events, 192.6 us)
Async XLA Ops:
  0.6 62.7 %collective-permute-start.6 = (bf16[64,3584]{1,0:T(8,128)(2,1)}, bf16[64,3584]{1,0:T(8,128)(2,1)S(1)}, u32[]{:S(2)}, u32[]{:S(2)}) collective-permute-start(bf16[64,3584]{1,0:T(8,128)(2,1)} %param.6), channel_id=1, source_target_pairs={{24,16},{26,18},{28,20},{30,22},{16,8},{18,10},{20,12},{22,14},{8,... | collective-permute-start | bytes 1376264 | tf_op jit(solution)/shard_map/ppermute | solution.py:116
  4.7 59.2 %collective-permute-start.9 = (bf16[64,3584]{1,0:T(8,128)(2,1)}, bf16[64,3584]{1,0:T(8,128)(2,1)S(1)}, u32[]{:S(2)}, u32[]{:S(2)}) collective-permute-start(bf16[64,3584]{1,0:T(8,128)(2,1)} %param.6), channel_id=1, source_target_pairs={{0,8},{2,10},{4,12},{6,14},{8,16},{10,18},{12,20},{14,22},{16,24},... | collective-permute-start | bytes 1376264 | tf_op jit(solution)/shard_map/ppermute | solution.py:116
  8.2 60.5 %collective-permute-start.34 = (bf16[64,3584]{1,0:T(8,128)(2,1)}, bf16[64,3584]{1,0:T(8,128)(2,1)S(1)}, u32[]{:S(2)}, u32[]{:S(2)}) collective-permute-start(bf16[64,3584]{1,0:T(8,128)(2,1)} %param.9), channel_id=1, source_target_pairs={{24,16},{26,18},{28,20},{30,22},{16,8},{18,10},{20,12},{22,14},{8,... | collective-permute-start | bytes 1376264 | tf_op jit(solution)/shard_map/ppermute | solution.py:116
  16.5 25.1 %collective-permute-start.1 = (bf16[2,64,3584]{2,1,0:T(8,128)(2,1)S(1)}, bf16[2,64,3584]{2,1,0:T(8,128)(2,1)S(1)}, u32[]{:S(2)}, u32[]{:S(2)}) collective-permute-start(bf16[2,64,3584]{2,1,0:T(8,128)(2,1)S(1)} %pad_maximum_fusion.4), channel_id=1, source_target_pairs={{0,4},{2,6},{4,0},{6,2},{8,12},{10,14},{12,8},{14,10},{16,20},{18,... | collective-permute-start | bytes 2752520 | tf_op jit(solution)/shard_map/ppermute | solution.py:112
  24.3 45.0 %collective-permute-start.37 = (bf16[64,3584]{1,0:T(8,128)(2,1)S(1)}, bf16[64,3584]{1,0:T(8,128)(2,1)S(1)}, u32[]{:S(2)}, u32[]{:S(2)}) collective-permute-start(bf16[64,3584]{1,0:T(8,128)(2,1)S(1)} %copy-done.1), channel_id=1, source_target_pairs={{0,8},{2,10},{4,12},{6,14},{8,16},{10,18},{12,20},{14,22},{16,24},... | collective-permute-start | bytes 1376264 | tf_op jit(solution)/shard_map/ppermute | solution.py:116
  41.6 20.0 %collective-permute-start.31 = (bf16[2,64,3584]{2,1,0:T(8,128)(2,1)S(1)}, bf16[2,64,3584]{2,1,0:T(8,128)(2,1)S(1)}, u32[]{:S(2)}, u32[]{:S(2)}) collective-permute-start(bf16[2,64,3584]{2,1,0:T(8,128)(2,1)S(1)} %pad_maximum_fusion.12), channel_id=1, source_target_pairs={{0,2},{2,0},{4,6},{6,4},{8,10},{10,8},{12,14},{14,12},{16,18},{18,... | collective-permute-start | bytes 2752520 | tf_op jit(solution)/shard_map/ppermute | solution.py:112
  61.7 97.5 %collective-permute-start.2 = (bf16[3584,512]{1,0:T(8,128)(2,1)S(1)}, bf16[3584,512]{1,0:T(8,128)(2,1)S(1)}, u32[]{:S(2)}, u32[]{:S(2)}) collective-permute-start(bf16[3584,512]{1,0:T(8,128)(2,1)S(1)} %bitcast.284), channel_id=1, source_target_pairs={{0,1},{1,0},{2,3},{3,2},{4,5},{5,4},{6,7},{7,6},{8,9},{9,8},{10,11... | collective-permute-start | bytes 11010056 | tf_op jit(solution)/shard_map/ppermute | solution.py:207
  63.3 103.4 %collective-permute-start.3 = (bf16[512,3584]{1,0:T(8,128)(2,1)S(1)}, bf16[512,3584]{1,0:T(8,128)(2,1)S(1)}, u32[]{:S(2)}, u32[]{:S(2)}) collective-permute-start(bf16[512,3584]{1,0:T(8,128)(2,1)S(1)} %bitcast.293), channel_id=1, source_target_pairs={{0,1},{1,0},{2,3},{3,2},{4,5},{5,4},{6,7},{7,6},{8,9},{9,8},{10,11... | collective-permute-start | bytes 11010056 | tf_op jit(solution)/shard_map/ppermute | solution.py:208
  63.9 63.0 %collective-permute-start.7 = (bf16[64,3584]{1,0:T(8,128)(2,1)S(1)}, bf16[64,3584]{1,0:T(8,128)(2,1)}, u32[]{:S(2)}, u32[]{:S(2)}) collective-permute-start(bf16[64,3584]{1,0:T(8,128)(2,1)S(1)} %collective-permute-done.6), channel_id=1, source_target_pairs={{16,8},{18,10},{20,12},{22,14},{8,0},{10,2},{12,4},{14,6},{17,9},{... | collective-permute-start | bytes 1376264 | tf_op jit(solution)/shard_map/ppermute | solution.py:116
  81.0 21.2 %collective-permute-start.17 = (bf16[2,64,3584]{2,1,0:T(8,128)(2,1)S(1)}, bf16[2,64,3584]{2,1,0:T(8,128)(2,1)S(1)}, u32[]{:S(2)}, u32[]{:S(2)}) collective-permute-start(bf16[2,64,3584]{2,1,0:T(8,128)(2,1)S(1)} %pad_maximum_fusion.8), channel_id=1, source_target_pairs={{0,4},{2,6},{4,0},{6,2},{8,12},{10,14},{12,8},{14,10},{16,20},{18,... | collective-permute-start | bytes 2752520 | tf_op jit(solution)/shard_map/ppermute | solution.py:112
  82.4 46.4 %collective-permute-start.10 = (bf16[64,3584]{1,0:T(8,128)(2,1)S(1)}, bf16[64,3584]{1,0:T(8,128)(2,1)}, u32[]{:S(2)}, u32[]{:S(2)}) collective-permute-start(bf16[64,3584]{1,0:T(8,128)(2,1)S(1)} %copy-done.15), channel_id=1, source_target_pairs={{8,16},{10,18},{12,20},{14,22},{16,24},{18,26},{20,28},{22,30},{9,... | collective-permute-start | bytes 1376264 | tf_op jit(solution)/shard_map/ppermute | solution.py:116
  102.2 20.2 %collective-permute-start.45 = (bf16[2,64,3584]{2,1,0:T(8,128)(2,1)S(1)}, bf16[2,64,3584]{2,1,0:T(8,128)(2,1)S(1)}, u32[]{:S(2)}, u32[]{:S(2)}) collective-permute-start(bf16[2,64,3584]{2,1,0:T(8,128)(2,1)S(1)} %pad_maximum_fusion.16), channel_id=1, source_target_pairs={{0,2},{2,0},{4,6},{6,4},{8,10},{10,8},{12,14},{14,12},{16,18},{18,... | collective-permute-start | bytes 2752520 | tf_op jit(solution)/shard_map/ppermute | solution.py:112
  128.8 54.3 %collective-permute-start.8 = (bf16[64,3584]{1,0:T(8,128)(2,1)}, bf16[64,3584]{1,0:T(8,128)(2,1)}, u32[]{:S(2)}, u32[]{:S(2)}) collective-permute-start(bf16[64,3584]{1,0:T(8,128)(2,1)} %collective-permute-done.7), channel_id=1, source_target_pairs={{8,0},{10,2},{12,4},{14,6},{9,1},{11,3},{13,5},{15,7}} | collective-permute-start | bytes 1376264 | tf_op jit(solution)/shard_map/ppermute | solution.py:116
  133.1 50.0 %collective-permute-start.11 = (bf16[64,3584]{1,0:T(8,128)(2,1)}, bf16[64,3584]{1,0:T(8,128)(2,1)}, u32[]{:S(2)}, u32[]{:S(2)}) collective-permute-start(bf16[64,3584]{1,0:T(8,128)(2,1)} %collective-permute-done.10), channel_id=1, source_target_pairs={{16,24},{18,26},{20,28},{22,30},{17,25},{19,27},{21,29},{23,31}} | collective-permute-start | bytes 1376264 | tf_op jit(solution)/shard_map/ppermute | solution.py:116
  156.7 46.3 %collective-permute-start.36 = (bf16[64,3584]{1,0:T(8,128)(2,1)}, bf16[64,3584]{1,0:T(8,128)(2,1)}, u32[]{:S(2)}, u32[]{:S(2)}) collective-permute-start(bf16[64,3584]{1,0:T(8,128)(2,1)} %collective-permute-done.35), channel_id=1, source_target_pairs={{8,0},{10,2},{12,4},{14,6},{9,1},{11,3},{13,5},{15,7}} | collective-permute-start | bytes 1376264 | tf_op jit(solution)/shard_map/ppermute | solution.py:116
  159.2 43.9 %collective-permute-start.39 = (bf16[64,3584]{1,0:T(8,128)(2,1)}, bf16[64,3584]{1,0:T(8,128)(2,1)}, u32[]{:S(2)}, u32[]{:S(2)}) collective-permute-start(bf16[64,3584]{1,0:T(8,128)(2,1)} %collective-permute-done.38), channel_id=1, source_target_pairs={{16,24},{18,26},{20,28},{22,30},{17,25},{19,27},{21,29},{23,31}} | collective-permute-start | bytes 1376264 | tf_op jit(solution)/shard_map/ppermute | solution.py:116
  185.5 24.3 %collective-permute-start.12 = (bf16[64,3584]{1,0:T(8,128)(2,1)}, bf16[64,3584]{1,0:T(8,128)(2,1)S(1)}, u32[]{:S(2)}, u32[]{:S(2)}) collective-permute-start(bf16[64,3584]{1,0:T(8,128)(2,1)} %get-tuple-element.14), channel_id=1, source_target_pairs={{0,2},{2,0},{4,6},{6,4},{8,10},{10,8},{12,14},{14,12},{16,18},{18,... | collective-permute-start | bytes 1376264 | tf_op jit(solution)/shard_map/ppermute | solution.py:112
  316.4 66.4 %collective-permute-start.32 = (bf16[2,64,3584]{2,1,0:T(8,128)(2,1)S(1)}, bf16[2,64,3584]{2,1,0:T(8,128)(2,1)}, u32[]{:S(2)}, u32[]{:S(2)}) collective-permute-start(bf16[2,64,3584]{2,1,0:T(8,128)(2,1)S(1)} %pad_maximum_fusion.13), channel_id=1, source_target_pairs={{0,2},{2,0},{4,6},{6,4},{8,10},{10,8},{12,14},{14,12},{16,18},{18,... | collective-permute-start | bytes 2752520 | tf_op jit(solution)/shard_map/ppermute | solution.py:112
  325.2 60.8 %collective-permute-start.46 = (bf16[2,64,3584]{2,1,0:T(8,128)(2,1)}, bf16[2,64,3584]{2,1,0:T(8,128)(2,1)}, u32[]{:S(2)}, u32[]{:S(2)}) collective-permute-start(bf16[2,64,3584]{2,1,0:T(8,128)(2,1)} %pad_maximum_fusion.17), channel_id=1, source_target_pairs={{0,2},{2,0},{4,6},{6,4},{8,10},{10,8},{12,14},{14,12},{16,18},{18,... | collective-permute-start | bytes 2752520 | tf_op jit(solution)/shard_map/ppermute | solution.py:112
  339.4 47.9 %collective-permute-start.50 = (bf16[2,64,3584]{2,1,0:T(8,128)(2,1)S(1)}, bf16[2,64,3584]{2,1,0:T(8,128)(2,1)S(1)}, u32[]{:S(2)}, u32[]{:S(2)}) collective-permute-start(bf16[2,64,3584]{2,1,0:T(8,128)(2,1)S(1)} %pad_maximum_fusion.19), channel_id=1, source_target_pairs={{0,2},{2,0},{4,6},{6,4},{8,10},{10,8},{12,14},{14,12},{16,18},{18,... | collective-permute-start | bytes 2752520 | tf_op jit(solution)/shard_map/ppermute | solution.py:112
  340.1 49.3 %collective-permute-start.42 = (bf16[2,64,3584]{2,1,0:T(8,128)(2,1)S(1)}, bf16[2,64,3584]{2,1,0:T(8,128)(2,1)}, u32[]{:S(2)}, u32[]{:S(2)}) collective-permute-start(bf16[2,64,3584]{2,1,0:T(8,128)(2,1)S(1)} %pad_maximum_fusion.15), channel_id=1, source_target_pairs={{0,2},{2,0},{4,6},{6,4},{8,10},{10,8},{12,14},{14,12},{16,18},{18,... | collective-permute-start | bytes 2752520 | tf_op jit(solution)/shard_map/ppermute | solution.py:112
  346.1 44.5 %collective-permute-start.4 = (bf16[2,64,3584]{2,1,0:T(8,128)(2,1)S(1)}, bf16[2,64,3584]{2,1,0:T(8,128)(2,1)}, u32[]{:S(2)}, u32[]{:S(2)}) collective-permute-start(bf16[2,64,3584]{2,1,0:T(8,128)(2,1)S(1)} %pad_maximum_fusion.5), channel_id=1, source_target_pairs={{0,4},{2,6},{4,0},{6,2},{8,12},{10,14},{12,8},{14,10},{16,20},{18,... | collective-permute-start | bytes 2752520 | tf_op jit(solution)/shard_map/ppermute | solution.py:112
  382.8 20.0 %collective-permute-start.18 = (bf16[2,64,3584]{2,1,0:T(8,128)(2,1)S(1)}, bf16[2,64,3584]{2,1,0:T(8,128)(2,1)S(1)}, u32[]{:S(2)}, u32[]{:S(2)}) collective-permute-start(bf16[2,64,3584]{2,1,0:T(8,128)(2,1)S(1)} %pad_maximum_fusion.9), channel_id=1, source_target_pairs={{0,4},{2,6},{4,0},{6,2},{8,12},{10,14},{12,8},{14,10},{16,20},{18,... | collective-permute-start | bytes 2752520 | tf_op jit(solution)/shard_map/ppermute | solution.py:112
  386.0 42.6 %collective-permute-start.22 = (bf16[2,64,3584]{2,1,0:T(8,128)(2,1)S(1)}, bf16[2,64,3584]{2,1,0:T(8,128)(2,1)S(1)}, u32[]{:S(2)}, u32[]{:S(2)}) collective-permute-start(bf16[2,64,3584]{2,1,0:T(8,128)(2,1)S(1)} %pad_maximum_fusion.11), channel_id=1, source_target_pairs={{0,4},{2,6},{4,0},{6,2},{8,12},{10,14},{12,8},{14,10},{16,20},{18,... | collective-permute-start | bytes 2752520 | tf_op jit(solution)/shard_map/ppermute | solution.py:112
  387.3 41.1 %collective-permute-start.14 = (bf16[2,64,3584]{2,1,0:T(8,128)(2,1)S(1)}, bf16[2,64,3584]{2,1,0:T(8,128)(2,1)S(1)}, u32[]{:S(2)}, u32[]{:S(2)}) collective-permute-start(bf16[2,64,3584]{2,1,0:T(8,128)(2,1)S(1)} %pad_maximum_fusion.7), channel_id=1, source_target_pairs={{0,4},{2,6},{4,0},{6,2},{8,12},{10,14},{12,8},{14,10},{16,20},{18,... | collective-permute-start | bytes 2752520 | tf_op jit(solution)/shard_map/ppermute | solution.py:112
  389.4 135.7 %collective-permute-start.58 = (bf16[3584,512]{1,0:T(8,128)(2,1)S(1)}, bf16[3584,512]{1,0:T(8,128)(2,1)S(1)}, u32[]{:S(2)}, u32[]{:S(2)}) collective-permute-start(bf16[3584,512]{1,0:T(8,128)(2,1)S(1)} %copy-done.45), channel_id=1, source_target_pairs={{0,1},{1,0},{2,3},{3,2},{4,5},{5,4},{6,7},{7,6},{8,9},{9,8},{10,11... | collective-permute-start | bytes 11010056 | tf_op jit(solution)/shard_map/ppermute | solution.py:240
  390.6 143.3 %collective-permute-start.59 = (bf16[512,3584]{1,0:T(8,128)(2,1)}, bf16[512,3584]{1,0:T(8,128)(2,1)S(1)}, u32[]{:S(2)}, u32[]{:S(2)}) collective-permute-start(bf16[512,3584]{1,0:T(8,128)(2,1)} %convolution_convert_fusion), channel_id=1, source_target_pairs={{0,1},{1,0},{2,3},{3,2},{4,5},{5,4},{6,7},{7,6},{8,9},{9,8},{10,11... | collective-permute-start | bytes 11010056 | tf_op jit(solution)/shard_map/ppermute | solution.py:239
  402.8 42.1 %collective-permute-start.51 = (bf16[64,3584]{1,0:T(8,128)(2,1)S(1)}, bf16[64,3584]{1,0:T(8,128)(2,1)S(1)}, u32[]{:S(2)}, u32[]{:S(2)}) collective-permute-start(bf16[64,3584]{1,0:T(8,128)(2,1)S(1)} %fusion.102), channel_id=1, source_target_pairs={{0,4},{2,6},{4,0},{6,2},{8,12},{10,14},{12,8},{14,10},{16,20},{18,... | collective-permute-start | bytes 1376264 | tf_op jit(solution)/shard_map/ppermute | solution.py:112
  442.7 20.2 %collective-permute-start.55 = (bf16[64,3584]{1,0:T(8,128)(2,1)S(1)}, bf16[64,3584]{1,0:T(8,128)(2,1)S(1)}, u32[]{:S(2)}, u32[]{:S(2)}) collective-permute-start(bf16[64,3584]{1,0:T(8,128)(2,1)S(1)} %add_convert_fusion.7), channel_id=1, source_target_pairs={{24,16},{26,18},{28,20},{30,22},{25,17},{27,19},{29,21},{31,23}} | collective-permute-start | bytes 1376264 | tf_op jit(solution)/shard_map/ppermute | solution.py:116
  444.0 20.2 %collective-permute-start.52 = (bf16[64,3584]{1,0:T(8,128)(2,1)S(1)}, bf16[64,3584]{1,0:T(8,128)(2,1)S(1)}, u32[]{:S(2)}, u32[]{:S(2)}) collective-permute-start(bf16[64,3584]{1,0:T(8,128)(2,1)S(1)} %add_convert_fusion.7), channel_id=1, source_target_pairs={{0,8},{2,10},{4,12},{6,14},{1,9},{3,11},{5,13},{7,15}} | collective-permute-start | bytes 1376264 | tf_op jit(solution)/shard_map/ppermute | solution.py:116
  444.9 20.3 %collective-permute-start.23 = (bf16[64,3584]{1,0:T(8,128)(2,1)S(1)}, bf16[64,3584]{1,0:T(8,128)(2,1)S(1)}, u32[]{:S(2)}, u32[]{:S(2)}) collective-permute-start(bf16[64,3584]{1,0:T(8,128)(2,1)S(1)} %fusion.110), channel_id=1, source_target_pairs={{0,2},{2,0},{4,6},{6,4},{8,10},{10,8},{12,14},{14,12},{16,18},{18,... | collective-permute-start | bytes 1376264 | tf_op jit(solution)/shard_map/ppermute | solution.py:112
  465.2 18.8 %collective-permute-start.47 = (bf16[64,3584]{1,0:T(8,128)(2,1)S(1)}, bf16[64,3584]{1,0:T(8,128)(2,1)S(1)}, u32[]{:S(2)}, u32[]{:S(2)}) collective-permute-start(bf16[64,3584]{1,0:T(8,128)(2,1)S(1)} %fusion.104), channel_id=1, source_target_pairs={{0,4},{2,6},{4,0},{6,2},{8,12},{10,14},{12,8},{14,10},{16,20},{18,... | collective-permute-start | bytes 1376264 | tf_op jit(solution)/shard_map/ppermute | solution.py:112
  (74 other events, 1021.1 us)
where the time goes:
time: 548 us; the launch traced here: 543 us
  waiting for transfers between devices  226 us (41%)
  matrix products  101 us (18%)
  starting transfers between devices  82.1 us (15%)
  blocking collectives  67 us (12%)
  other arithmetic  35.1 us (6%)
  local copies, waits for them, and re-layouts  30.5 us (6%)
    ppermute x32, waiting for transfers between devices, swapped(): lax.ppermute(array, 'expert', tuple(((i, i ^ bit) for i in range(16))))  169 us
    ppermute x24, waiting for transfers between devices, shifted(): lax.ppermute(array, 'expert', tuple(((i, i + 4 * step) for z in senders f...  56.8 us
    ppermute x24, starting transfers between devices, shifted(): lax.ppermute(array, 'expert', tuple(((i, i + 4 * step) for z in senders f...  53.6 us
    dot_general x8, matrix products, transposed_dot(): lax.dot_general(rows, weights, (((1,), (1,)), ((), ())), preferred_elemen...  36.7 us
    dot_general x4, matrix products, outer(): lax.dot_general(rows, columns, (((0,), (0,)), ((), ())), preferred_elemen...  34.7 us
    all_gather x1, blocking collectives, dense_shards(): lax.all_gather(inner, 'expert', axis=0, tiled=True)  33.8 us
    all_gather x1, blocking collectives, dense_shards(): lax.all_gather(gate_of, 'expert', axis=0, tiled=True)  33.2 us
    ppermute x32, starting transfers between devices, swapped(): lax.ppermute(array, 'expert', tuple(((i, i ^ bit) for i in range(16))))  27.2 us
  transfers between devices with their start and end apart: 60, of which 27 were waited for; matrix products, arithmetic and copies ran while one was open for 25% of the time, Pallas kernels for 0%

commit v1 on v0

--- a/solution.py
+++ b/solution.py
@@ -5,6 +5,29 @@
 
 GELU_C = 0.7978845608028654
 GELU_A = 0.044715
+
+
+def wrap_the_units(v0, mesh_dim):
+    n_lanes = jax.lax.axis_size(mesh_dim)
+    in_order = []
+    rr = 0
+    while rr < n_lanes:
+        in_order.append((rr, (rr + 1) % n_lanes))
+        rr += 1
+    series = []
+    rr = 0
+    while rr < n_lanes:
+        series.append((rr, (rr - 1) % n_lanes))
+        rr += 1
+    v_now, big = ([v0], [v0])
+    for _ in range(n_lanes // 2):
+        v_now.append(jax.lax.ppermute(v_now[-1], axis_name=mesh_dim, perm=in_order))
+    idx = 0
+    while idx < (n_lanes - 1) // 2:
+        big.append(jax.lax.ppermute(big[-1], axis_name=mesh_dim, perm=series))
+        idx = idx + 1
+    new = jnp.concatenate([*v_now[::-1], *big[1:]], axis=0)
+    return jnp.roll(new, (jax.lax.axis_index(mesh_dim) - n_lanes // 2) * v0.shape[0], axis=0)
 
 
 def gelu_value(hidden):
@@ -225,9 +248,7 @@
     d_tokens = scattered_layers(dx_columns, layer)
     order = jnp.concatenate(sources)
     inner = jnp.zeros((owners, tok_rows), jnp.float32).at[order].set(jnp.concatenate(inners))
-    inner_all = lax.all_gather(inner, "expert", axis=0, tiled=True).reshape(
-        owners, owners, tok_rows
-    )
+    inner_all = wrap_the_units(inner, "expert").reshape(owners, owners, tok_rows)
     home = lax.dynamic_index_in_dim(inner_all, mine, axis=1, keepdims=False)
     d_gates = jnp.sum(jnp.where(named, home.T[:, None, :], 0.0), axis=2)
     all_x, all_u = (jnp.concatenate(slots_x), jnp.concatenate(slots_u))

time: 548 us -> 555 us (1.013)
  starting transfers between devices: 82.1 us -> 121 us
  blocking collectives: 67 us -> 46.4 us
  local copies, waits for them, and re-layouts: 30.5 us -> 17 us
  matrix products: 101 us -> 87.8 us
  waiting for transfers between devices: 226 us -> 233 us
    all_gather x1 -> x0, blocking collectives: 33.8 us -> none  [dense_shards(): lax.all_gather(inner, 'expert', axis=0, tiled=True)]
    ppermute x0 -> x15, starting transfers between devices: none -> 22.2 us  [the longest x7 11.7 us: wrap_the_units(): big.append(jax.lax.ppermute(big[-1], axis_name=mesh_dim, perm=series))]
    ppermute x0 -> x15, waiting for transfers between devices: none -> 15.2 us  [the longest x8 10.1 us: wrap_the_units(): v_now.append(jax.lax.ppermute(v_now[-1], axis_name=mesh_dim, perm=in_order))]
    unnamed x116 -> x159, local copies, waits for them, and re-layouts: 24 us -> 10.4 us
    all_gather x1, blocking collectives: 33.2 us -> 46.4 us  [dense_shards(): lax.all_gather(gate_of, 'expert', axis=0, tiled=True)]
    ppermute x24, waiting for transfers between devices: 56.8 us -> 43.6 us  [shifted(): lax.ppermute(array, 'expert', tuple(((i, i + 4 * step) for z in senders f...]
    ppermute x32, starting transfers between devices: 27.2 us -> 40.1 us  [swapped(): lax.ppermute(array, 'expert', tuple(((i, i ^ bit) for i in range(16))))]
    dot_general x4, matrix products: 18.9 us -> 12.2 us  [dense_shards(): out_part = jnp.dot(gated[s], down_full, preferred_element_type=jnp.float32)]
  transfers between devices with their start and end apart: 60 -> 75, of which waited for: 27 -> 40; matrix products, arithmetic and copies ran while one was open for 25% -> 21% of each run, Pallas kernels for 0% -> 0%
where the time goes in v1:
time: 555 us; the launch traced here: 547 us
  waiting for transfers between devices  233 us (42%)
  starting transfers between devices  121 us (22%)
  matrix products  87.8 us (16%)
  blocking collectives  46.4 us (8%)
  other arithmetic  38.3 us (7%)
  local copies, waits for them, and re-layouts  17 us (3%)
    ppermute x32, waiting for transfers between devices, swapped(): lax.ppermute(array, 'expert', tuple(((i, i ^ bit) for i in range(16))))  174 us
    ppermute x24, starting transfers between devices, shifted(): lax.ppermute(array, 'expert', tuple(((i, i + 4 * step) for z in senders f...  57.7 us
    all_gather x1, blocking collectives, dense_shards(): lax.all_gather(gate_of, 'expert', axis=0, tiled=True)  46.4 us
    ppermute x24, waiting for transfers between devices, shifted(): lax.ppermute(array, 'expert', tuple(((i, i + 4 * step) for z in senders f...  43.6 us
    ppermute x32, starting transfers between devices, swapped(): lax.ppermute(array, 'expert', tuple(((i, i ^ bit) for i in range(16))))  40.1 us
    dot_general x8, matrix products, transposed_dot(): lax.dot_general(rows, weights, (((1,), (1,)), ((), ())), preferred_elemen...  32.3 us
    dot_general x4, matrix products, outer(): lax.dot_general(rows, columns, (((0,), (0,)), ((), ())), preferred_elemen...  29.6 us
    convert_element_type x16, other arithmetic, add_rows(): return total.astype(jnp.bfloat16)  15 us
  transfers between devices with their start and end apart: 75, of which 40 were waited for; matrix products, arithmetic and copies ran while one was open for 21% of the time, Pallas kernels for 0%

profile of v1, /device:TPU:20, one launch (start us, length us, event | category | flops | bytes accessed | tf_op | source)
XLA Modules:
  0.0 546.5 jit_solution(10034245544902155205)
XLA Ops:
  17.1 7.2 %collective-permute-done.30 = bf16[64,3584]{1,0:T(8,128)(2,1)S(1)} collective-permute-done((bf16[64,3584]{1,0:T(8,128)(2,1)}, bf16[64,3584]{1,0:T(8,128)(2,1)S(1)}, u32[]{:S(2)}, u32[]{:S(2)}) %collective-permute-start.30) | collective-permute-done | bytes 458784 | tf_op jit(solution)/shard_map/ppermute | solution.py:135
  27.9 13.7 %collective-permute-done.1 = bf16[2,64,3584]{2,1,0:T(8,128)(2,1)S(1)} collective-permute-done((bf16[2,64,3584]{2,1,0:T(8,128)(2,1)S(1)}, bf16[2,64,3584]{2,1,0:T(8,128)(2,1)S(1)}, u32[]{:S(2)}, u32[]{:S(2)}) %collective-permute-start.1) | collective-permute-done | bytes 917536 | tf_op jit(solution)/shard_map/ppermute | solution.py:135
  42.2 19.4 %collective-permute-done.31 = bf16[2,64,3584]{2,1,0:T(8,128)(2,1)S(1)} collective-permute-done((bf16[2,64,3584]{2,1,0:T(8,128)(2,1)S(1)}, bf16[2,64,3584]{2,1,0:T(8,128)(2,1)S(1)}, u32[]{:S(2)}, u32[]{:S(2)}) %collective-permute-start.31) | collective-permute-done | bytes 917536 | tf_op jit(solution)/shard_map/ppermute | solution.py:135
  67.3 10.7 %collective-permute-done.16 = bf16[64,3584]{1,0:T(8,128)(2,1)S(1)} collective-permute-done((bf16[64,3584]{1,0:T(8,128)(2,1)S(1)}, bf16[64,3584]{1,0:T(8,128)(2,1)S(1)}, u32[]{:S(2)}, u32[]{:S(2)}) %collective-permute-start.16) | collective-permute-done | bytes 458784 | tf_op jit(solution)/shard_map/ppermute | solution.py:135
  80.9 18.4 %collective-permute-done.17 = bf16[2,64,3584]{2,1,0:T(8,128)(2,1)S(1)} collective-permute-done((bf16[2,64,3584]{2,1,0:T(8,128)(2,1)S(1)}, bf16[2,64,3584]{2,1,0:T(8,128)(2,1)S(1)}, u32[]{:S(2)}, u32[]{:S(2)}) %collective-permute-start.17) | collective-permute-done | bytes 917536 | tf_op jit(solution)/shard_map/ppermute | solution.py:135
  99.9 19.6 %collective-permute-done.45 = bf16[2,64,3584]{2,1,0:T(8,128)(2,1)S(1)} collective-permute-done((bf16[2,64,3584]{2,1,0:T(8,128)(2,1)S(1)}, bf16[2,64,3584]{2,1,0:T(8,128)(2,1)S(1)}, u32[]{:S(2)}, u32[]{:S(2)}) %collective-permute-start.45) | collective-permute-done | bytes 917536 | tf_op jit(solution)/shard_map/ppermute | solution.py:135
  131.1 4.3 collective-permute-done.38
  138.2 5.7 %collective-permute-done.20 = bf16[64,3584]{1,0:T(8,128)(2,1)S(1)} collective-permute-done((bf16[64,3584]{1,0:T(8,128)(2,1)S(1)}, bf16[64,3584]{1,0:T(8,128)(2,1)S(1)}, u32[]{:S(2)}, u32[]{:S(2)}) %collective-permute-start.20) | collective-permute-done | bytes 458784 | tf_op jit(solution)/shard_map/ppermute | solution.py:135
  145.5 6.9 %collective-permute-done.48 = bf16[64,3584]{1,0:T(8,128)(2,1)S(1)} collective-permute-done((bf16[64,3584]{1,0:T(8,128)(2,1)S(1)}, bf16[64,3584]{1,0:T(8,128)(2,1)S(1)}, u32[]{:S(2)}, u32[]{:S(2)}) %collective-permute-start.48) | collective-permute-done | bytes 458784 | tf_op jit(solution)/shard_map/ppermute | solution.py:135
  154.9 5.8 %collective-permute-start.39 = (bf16[64,3584]{1,0:T(8,128)(2,1)}, bf16[64,3584]{1,0:T(8,128)(2,1)}, u32[]{:S(2)}, u32[]{:S(2)}) collective-permute-start(bf16[64,3584]{1,0:T(8,128)(2,1)} %collective-permute-done.38), channel_id=1, source_target_pairs={{16,24},{18,26},{20,28},{22,30},{17,25},{19,27},{21,29},{23,31}} | collective-permute-start | bytes 1376264 | tf_op jit(solution)/shard_map/ppermute | solution.py:139
  166.6 5.2 fusion.18
  171.9 6.7 %multiply_reduce_fusion.2 = (f32[256]{0:T(256)S(1)}, f32[256,1024]{1,0:T(8,128)}) fusion(f32[256,1024]{1,0:T(8,128)} %fusion.18, bf16[512,3584]{1,0:T(8,128)(2,1)} %copy-done.43, bf16[512,3584]{1,0:T(8,128)(2,1)} %bitcast.292, bf16[64,3584]{1,0:T(8,128)(2,1)} %get-tuple-element.58, bf16[64,3584]{1,0:T(8,128)(2,1)S(1)} %collective-permute-done.44, ...), kind=kOutput, calls=%fused_computation.133 | convolution fusion | flops 1903689472 | bytes 11273216 | tf_op jit(solution)/shard_map/dot_general | solution.py:196
  184.4 12.5 %collective-permute-done.49 = bf16[2,64,3584]{2,1,0:T(8,128)(2,1)S(1)} collective-permute-done((bf16[2,64,3584]{2,1,0:T(8,128)(2,1)}, bf16[2,64,3584]{2,1,0:T(8,128)(2,1)S(1)}, u32[]{:S(2)}, u32[]{:S(2)}) %collective-permute-start.49) | collective-permute-done | bytes 917536 | tf_op jit(solution)/shard_map/ppermute | solution.py:135
  212.5 7.6 %collective-permute-done.13 = bf16[2,64,3584]{2,1,0:T(8,128)(2,1)S(1)} collective-permute-done((bf16[2,64,3584]{2,1,0:T(8,128)(2,1)}, bf16[2,64,3584]{2,1,0:T(8,128)(2,1)S(1)}, u32[]{:S(2)}, u32[]{:S(2)}) %collective-permute-start.13) | collective-permute-done | bytes 917536 | tf_op jit(solution)/shard_map/ppermute | solution.py:135
  220.2 5.0 collective-permute-done.41
  225.3 4.3 fusion.10
  229.6 4.8 multiply_reduce_fusion
  278.6 46.4 %all-gather = f32[16,64,16]{1,2,0:T(8,128)S(1)} all-gather(f32[1,64,16]{1,2,0:T(8,128)S(1)} %bitcast.281), channel_id=1, replica_groups=mesh['expert'=16,'tok'=2] {'expert'}, dimensions={0}, use_global_device_ids=true | all-gather | bytes 69632 | tf_op jit(solution)/shard_map/all_gather | solution.py:217
  329.6 5.4 convolution_convert_fusion.5
  347.2 4.3 convolution_convert_fusion.2
  364.0 5.4 convolution_convert_fusion.6
  371.6 5.9 %convolution_convert_fusion = bf16[512,3584]{1,0:T(8,128)(2,1)} fusion(bf16[1024,3584]{1,0:T(8,128)(2,1)S(1)} %bitcast.260, bf16[1024,1024]{1,0:T(8,128)(2,1)S(1)} %pad_maximum_fusion.3), kind=kOutput, calls=%fused_computation.9 | convolution fusion | flops 3759931392 | bytes 12058624 | tf_op jit(solution)/shard_map/dot_general | solution.py:202
  377.5 8.6 %convolution_convert_fusion.1 = bf16[3584,512]{1,0:T(8,128)(2,1)} fusion(bf16[1024,3584]{1,0:T(8,128)(2,1)} %constant_dynamic-update-slice_fusion.32, bf16[1024,1024]{1,0:T(8,128)(2,1)S(1)} %pad_maximum_fusion.2), kind=kOutput, calls=%fused_computation.10 | convolution fusion | flops 3759931392 | bytes 12058624 | tf_op jit(solution)/shard_map/dot_general | solution.py:202
  396.6 13.0 %collective-permute-done.18 = bf16[2,64,3584]{2,1,0:T(8,128)(2,1)S(1)} collective-permute-done((bf16[2,64,3584]{2,1,0:T(8,128)(2,1)}, bf16[2,64,3584]{2,1,0:T(8,128)(2,1)S(1)}, u32[]{:S(2)}, u32[]{:S(2)}) %collective-permute-start.18) | collective-permute-done | bytes 917536 | tf_op jit(solution)/shard_map/ppermute | solution.py:135
  411.7 23.6 %collective-permute-done.14 = bf16[2,64,3584]{2,1,0:T(8,128)(2,1)S(1)} collective-permute-done((bf16[2,64,3584]{2,1,0:T(8,128)(2,1)}, bf16[2,64,3584]{2,1,0:T(8,128)(2,1)S(1)}, u32[]{:S(2)}, u32[]{:S(2)}) %collective-permute-start.14) | collective-permute-done | bytes 917536 | tf_op jit(solution)/shard_map/ppermute | solution.py:135
  438.6 8.5 %collective-permute-done.43 = bf16[64,3584]{1,0:T(8,128)(2,1)S(1)} collective-permute-done((bf16[64,3584]{1,0:T(8,128)(2,1)S(1)}, bf16[64,3584]{1,0:T(8,128)(2,1)S(1)}, u32[]{:S(2)}, u32[]{:S(2)}) %collective-permute-start.43) | collective-permute-done | bytes 458784 | tf_op jit(solution)/shard_map/ppermute | solution.py:135
  451.5 16.5 %collective-permute-done.55 = bf16[64,3584]{1,0:T(8,128)(2,1)S(1)} collective-permute-done((bf16[64,3584]{1,0:T(8,128)(2,1)S(1)}, bf16[64,3584]{1,0:T(8,128)(2,1)S(1)}, u32[]{:S(2)}, u32[]{:S(2)}) %collective-permute-start.55) | collective-permute-done | bytes 458784 | tf_op jit(solution)/shard_map/ppermute | solution.py:139
  474.7 7.2 %collective-permute-done.27 = bf16[64,3584]{1,0:T(8,128)(2,1)S(1)} collective-permute-done((bf16[64,3584]{1,0:T(8,128)(2,1)S(1)}, bf16[64,3584]{1,0:T(8,128)(2,1)S(1)}, u32[]{:S(2)}, u32[]{:S(2)}) %collective-permute-start.27) | collective-permute-done | bytes 458784 | tf_op jit(solution)/shard_map/ppermute | solution.py:139
  483.2 4.6 collective-permute-start.56
  493.6 3.9 collective-permute-done.56
  530.9 9.4 %fusion = bf16[1,3584,512]{2,1,0:T(8,128)(2,1)} fusion(bf16[3584,512]{1,0:T(8,128)(2,1)} %collective-permute-done.73, bf16[1024,3584]{1,0:T(8,128)(2,1)} %constant_dynamic-update-slice_fusion.32, bf16[1024,1024]{1,0:T(8,128)(2,1)S(1)} %pad_maximum_fusion.2), kind=kOutput, calls=%fused_computation.11 | convolution fusion | flops 3763601408 | bytes 15728640 | tf_op jit(solution)/shard_map/dot_general | solution.py:202
  540.4 5.7 %fusion.1 = bf16[1,512,3584]{2,1,0:T(8,128)(2,1)} fusion(bf16[512,3584]{1,0:T(8,128)(2,1)S(1)} %collective-permute-done.74, bf16[1024,3584]{1,0:T(8,128)(2,1)S(1)} %bitcast.260, bf16[1024,1024]{1,0:T(8,128)(2,1)S(1)} %pad_maximum_fusion.3), kind=kOutput, calls=%fused_computation.12 | convolution fusion | flops 3763601408 | bytes 15728640 | tf_op jit(solution)/shard_map/dot_general | solution.py:202
  (387 shorter events, 217.7 us)
Async XLA Ops:
  0.6 61.1 %collective-permute-start.6 = (bf16[64,3584]{1,0:T(8,128)(2,1)}, bf16[64,3584]{1,0:T(8,128)(2,1)S(1)}, u32[]{:S(2)}, u32[]{:S(2)}) collective-permute-start(bf16[64,3584]{1,0:T(8,128)(2,1)} %param.6), channel_id=1, source_target_pairs={{24,16},{26,18},{28,20},{30,22},{16,8},{18,10},{20,12},{22,14},{8,... | collective-permute-start | bytes 1376264 | tf_op jit(solution)/shard_map/ppermute | solution.py:139
  4.7 57.7 %collective-permute-start.9 = (bf16[64,3584]{1,0:T(8,128)(2,1)}, bf16[64,3584]{1,0:T(8,128)(2,1)S(1)}, u32[]{:S(2)}, u32[]{:S(2)}) collective-permute-start(bf16[64,3584]{1,0:T(8,128)(2,1)} %param.6), channel_id=1, source_target_pairs={{0,8},{2,10},{4,12},{6,14},{8,16},{10,18},{12,20},{14,22},{16,24},... | collective-permute-start | bytes 1376264 | tf_op jit(solution)/shard_map/ppermute | solution.py:139
  8.2 57.5 %collective-permute-start.34 = (bf16[64,3584]{1,0:T(8,128)(2,1)}, bf16[64,3584]{1,0:T(8,128)(2,1)S(1)}, u32[]{:S(2)}, u32[]{:S(2)}) collective-permute-start(bf16[64,3584]{1,0:T(8,128)(2,1)} %param.9), channel_id=1, source_target_pairs={{24,16},{26,18},{28,20},{30,22},{16,8},{18,10},{20,12},{22,14},{8,... | collective-permute-start | bytes 1376264 | tf_op jit(solution)/shard_map/ppermute | solution.py:139
  16.5 25.1 %collective-permute-start.1 = (bf16[2,64,3584]{2,1,0:T(8,128)(2,1)S(1)}, bf16[2,64,3584]{2,1,0:T(8,128)(2,1)S(1)}, u32[]{:S(2)}, u32[]{:S(2)}) collective-permute-start(bf16[2,64,3584]{2,1,0:T(8,128)(2,1)S(1)} %pad_maximum_fusion.4), channel_id=1, source_target_pairs={{0,4},{2,6},{4,0},{6,2},{8,12},{10,14},{12,8},{14,10},{16,20},{18,... | collective-permute-start | bytes 2752520 | tf_op jit(solution)/shard_map/ppermute | solution.py:135
  24.3 42.0 %collective-permute-start.37 = (bf16[64,3584]{1,0:T(8,128)(2,1)S(1)}, bf16[64,3584]{1,0:T(8,128)(2,1)S(1)}, u32[]{:S(2)}, u32[]{:S(2)}) collective-permute-start(bf16[64,3584]{1,0:T(8,128)(2,1)S(1)} %copy-done.2), channel_id=1, source_target_pairs={{0,8},{2,10},{4,12},{6,14},{8,16},{10,18},{12,20},{14,22},{16,24},... | collective-permute-start | bytes 1376264 | tf_op jit(solution)/shard_map/ppermute | solution.py:139
  41.6 20.0 %collective-permute-start.31 = (bf16[2,64,3584]{2,1,0:T(8,128)(2,1)S(1)}, bf16[2,64,3584]{2,1,0:T(8,128)(2,1)S(1)}, u32[]{:S(2)}, u32[]{:S(2)}) collective-permute-start(bf16[2,64,3584]{2,1,0:T(8,128)(2,1)S(1)} %pad_maximum_fusion.12), channel_id=1, source_target_pairs={{0,2},{2,0},{4,6},{6,4},{8,10},{10,8},{12,14},{14,12},{16,18},{18,... | collective-permute-start | bytes 2752520 | tf_op jit(solution)/shard_map/ppermute | solution.py:135
  61.7 93.2 %collective-permute-start.2 = (bf16[3584,512]{1,0:T(8,128)(2,1)S(1)}, bf16[3584,512]{1,0:T(8,128)(2,1)S(1)}, u32[]{:S(2)}, u32[]{:S(2)}) collective-permute-start(bf16[3584,512]{1,0:T(8,128)(2,1)S(1)} %bitcast.284), channel_id=1, source_target_pairs={{0,1},{1,0},{2,3},{3,2},{4,5},{5,4},{6,7},{7,6},{8,9},{9,8},{10,11... | collective-permute-start | bytes 11010056 | tf_op jit(solution)/shard_map/ppermute | solution.py:230
  61.8 101.0 %collective-permute-start.3 = (bf16[512,3584]{1,0:T(8,128)(2,1)S(1)}, bf16[512,3584]{1,0:T(8,128)(2,1)S(1)}, u32[]{:S(2)}, u32[]{:S(2)}) collective-permute-start(bf16[512,3584]{1,0:T(8,128)(2,1)S(1)} %bitcast.294), channel_id=1, source_target_pairs={{0,1},{1,0},{2,3},{3,2},{4,5},{5,4},{6,7},{7,6},{8,9},{9,8},{10,11... | collective-permute-start | bytes 11010056 | tf_op jit(solution)/shard_map/ppermute | solution.py:231
  62.4 60.2 %collective-permute-start.7 = (bf16[64,3584]{1,0:T(8,128)(2,1)S(1)}, bf16[64,3584]{1,0:T(8,128)(2,1)}, u32[]{:S(2)}, u32[]{:S(2)}) collective-permute-start(bf16[64,3584]{1,0:T(8,128)(2,1)S(1)} %collective-permute-done.6), channel_id=1, source_target_pairs={{16,8},{18,10},{20,12},{22,14},{8,0},{10,2},{12,4},{14,6},{17,9},{... | collective-permute-start | bytes 1376264 | tf_op jit(solution)/shard_map/ppermute | solution.py:139
  78.1 21.2 %collective-permute-start.17 = (bf16[2,64,3584]{2,1,0:T(8,128)(2,1)S(1)}, bf16[2,64,3584]{2,1,0:T(8,128)(2,1)S(1)}, u32[]{:S(2)}, u32[]{:S(2)}) collective-permute-start(bf16[2,64,3584]{2,1,0:T(8,128)(2,1)S(1)} %pad_maximum_fusion.8), channel_id=1, source_target_pairs={{0,4},{2,6},{4,0},{6,2},{8,12},{10,14},{12,8},{14,10},{16,20},{18,... | collective-permute-start | bytes 2752520 | tf_op jit(solution)/shard_map/ppermute | solution.py:135
  78.7 45.8 %collective-permute-start.10 = (bf16[64,3584]{1,0:T(8,128)(2,1)S(1)}, bf16[64,3584]{1,0:T(8,128)(2,1)}, u32[]{:S(2)}, u32[]{:S(2)}) collective-permute-start(bf16[64,3584]{1,0:T(8,128)(2,1)S(1)} %collective-permute-done.9), channel_id=1, source_target_pairs={{8,16},{10,18},{12,20},{14,22},{16,24},{18,26},{20,28},{22,30},{9,... | collective-permute-start | bytes 1376264 | tf_op jit(solution)/shard_map/ppermute | solution.py:139
  99.3 20.2 %collective-permute-start.45 = (bf16[2,64,3584]{2,1,0:T(8,128)(2,1)S(1)}, bf16[2,64,3584]{2,1,0:T(8,128)(2,1)S(1)}, u32[]{:S(2)}, u32[]{:S(2)}) collective-permute-start(bf16[2,64,3584]{2,1,0:T(8,128)(2,1)S(1)} %pad_maximum_fusion.16), channel_id=1, source_target_pairs={{0,2},{2,0},{4,6},{6,4},{8,10},{10,8},{12,14},{14,12},{16,18},{18,... | collective-permute-start | bytes 2752520 | tf_op jit(solution)/shard_map/ppermute | solution.py:135
  124.5 56.5 %collective-permute-start.8 = (bf16[64,3584]{1,0:T(8,128)(2,1)}, bf16[64,3584]{1,0:T(8,128)(2,1)}, u32[]{:S(2)}, u32[]{:S(2)}) collective-permute-start(bf16[64,3584]{1,0:T(8,128)(2,1)} %collective-permute-done.7), channel_id=1, source_target_pairs={{8,0},{10,2},{12,4},{14,6},{9,1},{11,3},{13,5},{15,7}} | collective-permute-start | bytes 1376264 | tf_op jit(solution)/shard_map/ppermute | solution.py:139
  129.1 51.9 %collective-permute-start.11 = (bf16[64,3584]{1,0:T(8,128)(2,1)}, bf16[64,3584]{1,0:T(8,128)(2,1)}, u32[]{:S(2)}, u32[]{:S(2)}) collective-permute-start(bf16[64,3584]{1,0:T(8,128)(2,1)} %collective-permute-done.10), channel_id=1, source_target_pairs={{16,24},{18,26},{20,28},{22,30},{17,25},{19,27},{21,29},{23,31}} | collective-permute-start | bytes 1376264 | tf_op jit(solution)/shard_map/ppermute | solution.py:139
  152.4 46.9 %collective-permute-start.36 = (bf16[64,3584]{1,0:T(8,128)(2,1)}, bf16[64,3584]{1,0:T(8,128)(2,1)}, u32[]{:S(2)}, u32[]{:S(2)}) collective-permute-start(bf16[64,3584]{1,0:T(8,128)(2,1)} %collective-permute-done.35), channel_id=1, source_target_pairs={{8,0},{10,2},{12,4},{14,6},{9,1},{11,3},{13,5},{15,7}} | collective-permute-start | bytes 1376264 | tf_op jit(solution)/shard_map/ppermute | solution.py:139
  154.9 44.5 %collective-permute-start.39 = (bf16[64,3584]{1,0:T(8,128)(2,1)}, bf16[64,3584]{1,0:T(8,128)(2,1)}, u32[]{:S(2)}, u32[]{:S(2)}) collective-permute-start(bf16[64,3584]{1,0:T(8,128)(2,1)} %collective-permute-done.38), channel_id=1, source_target_pairs={{16,24},{18,26},{20,28},{22,30},{17,25},{19,27},{21,29},{23,31}} | collective-permute-start | bytes 1376264 | tf_op jit(solution)/shard_map/ppermute | solution.py:139
  178.7 18.2 %collective-permute-start.49 = (bf16[2,64,3584]{2,1,0:T(8,128)(2,1)}, bf16[2,64,3584]{2,1,0:T(8,128)(2,1)S(1)}, u32[]{:S(2)}, u32[]{:S(2)}) collective-permute-start(bf16[2,64,3584]{2,1,0:T(8,128)(2,1)} %pad_maximum_fusion.18), channel_id=1, source_target_pairs={{0,2},{2,0},{4,6},{6,4},{8,10},{10,8},{12,14},{14,12},{16,18},{18,... | collective-permute-start | bytes 2752520 | tf_op jit(solution)/shard_map/ppermute | solution.py:135
  183.1 21.3 %collective-permute-start.12 = (bf16[64,3584]{1,0:T(8,128)(2,1)S(1)}, bf16[64,3584]{1,0:T(8,128)(2,1)S(1)}, u32[]{:S(2)}, u32[]{:S(2)}) collective-permute-start(bf16[64,3584]{1,0:T(8,128)(2,1)S(1)} %get-tuple-element.14), channel_id=1, source_target_pairs={{0,2},{2,0},{4,6},{6,4},{8,10},{10,8},{12,14},{14,12},{16,18},{18,... | collective-permute-start | bytes 1376264 | tf_op jit(solution)/shard_map/ppermute | solution.py:135
  335.2 50.9 %collective-permute-start.32 = (bf16[2,64,3584]{2,1,0:T(8,128)(2,1)S(1)}, bf16[2,64,3584]{2,1,0:T(8,128)(2,1)}, u32[]{:S(2)}, u32[]{:S(2)}) collective-permute-start(bf16[2,64,3584]{2,1,0:T(8,128)(2,1)S(1)} %pad_maximum_fusion.13), channel_id=1, source_target_pairs={{0,2},{2,0},{4,6},{6,4},{8,10},{10,8},{12,14},{14,12},{16,18},{18,... | collective-permute-start | bytes 2752520 | tf_op jit(solution)/shard_map/ppermute | solution.py:135
  341.2 48.0 %collective-permute-start.46 = (bf16[2,64,3584]{2,1,0:T(8,128)(2,1)S(1)}, bf16[2,64,3584]{2,1,0:T(8,128)(2,1)}, u32[]{:S(2)}, u32[]{:S(2)}) collective-permute-start(bf16[2,64,3584]{2,1,0:T(8,128)(2,1)S(1)} %pad_maximum_fusion.17), channel_id=1, source_target_pairs={{0,2},{2,0},{4,6},{6,4},{8,10},{10,8},{12,14},{14,12},{16,18},{18,... | collective-permute-start | bytes 2752520 | tf_op jit(solution)/shard_map/ppermute | solution.py:135
  352.6 37.9 %collective-permute-start.50 = (bf16[2,64,3584]{2,1,0:T(8,128)(2,1)}, bf16[2,64,3584]{2,1,0:T(8,128)(2,1)}, u32[]{:S(2)}, u32[]{:S(2)}) collective-permute-start(bf16[2,64,3584]{2,1,0:T(8,128)(2,1)} %pad_maximum_fusion.19), channel_id=1, source_target_pairs={{0,2},{2,0},{4,6},{6,4},{8,10},{10,8},{12,14},{14,12},{16,18},{18,... | collective-permute-start | bytes 2752520 | tf_op jit(solution)/shard_map/ppermute | solution.py:135
  354.6 39.1 %collective-permute-start.42 = (bf16[2,64,3584]{2,1,0:T(8,128)(2,1)}, bf16[2,64,3584]{2,1,0:T(8,128)(2,1)}, u32[]{:S(2)}, u32[]{:S(2)}) collective-permute-start(bf16[2,64,3584]{2,1,0:T(8,128)(2,1)} %pad_maximum_fusion.15), channel_id=1, source_target_pairs={{0,2},{2,0},{4,6},{6,4},{8,10},{10,8},{12,14},{14,12},{16,18},{18,... | collective-permute-start | bytes 2752520 | tf_op jit(solution)/shard_map/ppermute | solution.py:135
  359.0 35.9 %collective-permute-start.4 = (bf16[2,64,3584]{2,1,0:T(8,128)(2,1)}, bf16[2,64,3584]{2,1,0:T(8,128)(2,1)}, u32[]{:S(2)}, u32[]{:S(2)}) collective-permute-start(bf16[2,64,3584]{2,1,0:T(8,128)(2,1)} %pad_maximum_fusion.5), channel_id=1, source_target_pairs={{0,4},{2,6},{4,0},{6,2},{8,12},{10,14},{12,8},{14,10},{16,20},{18,... | collective-permute-start | bytes 2752520 | tf_op jit(solution)/shard_map/ppermute | solution.py:135
  386.1 23.5 %collective-permute-start.18 = (bf16[2,64,3584]{2,1,0:T(8,128)(2,1)}, bf16[2,64,3584]{2,1,0:T(8,128)(2,1)S(1)}, u32[]{:S(2)}, u32[]{:S(2)}) collective-permute-start(bf16[2,64,3584]{2,1,0:T(8,128)(2,1)} %pad_maximum_fusion.9), channel_id=1, source_target_pairs={{0,4},{2,6},{4,0},{6,2},{8,12},{10,14},{12,8},{14,10},{16,20},{18,... | collective-permute-start | bytes 2752520 | tf_op jit(solution)/shard_map/ppermute | solution.py:135
  389.3 47.9 %collective-permute-start.22 = (bf16[2,64,3584]{2,1,0:T(8,128)(2,1)S(1)}, bf16[2,64,3584]{2,1,0:T(8,128)(2,1)S(1)}, u32[]{:S(2)}, u32[]{:S(2)}) collective-permute-start(bf16[2,64,3584]{2,1,0:T(8,128)(2,1)S(1)} %pad_maximum_fusion.11), channel_id=1, source_target_pairs={{0,4},{2,6},{4,0},{6,2},{8,12},{10,14},{12,8},{14,10},{16,20},{18,... | collective-permute-start | bytes 2752520 | tf_op jit(solution)/shard_map/ppermute | solution.py:135
  390.5 44.8 %collective-permute-start.14 = (bf16[2,64,3584]{2,1,0:T(8,128)(2,1)}, bf16[2,64,3584]{2,1,0:T(8,128)(2,1)S(1)}, u32[]{:S(2)}, u32[]{:S(2)}) collective-permute-start(bf16[2,64,3584]{2,1,0:T(8,128)(2,1)} %pad_maximum_fusion.7), channel_id=1, source_target_pairs={{0,4},{2,6},{4,0},{6,2},{8,12},{10,14},{12,8},{14,10},{16,20},{18,... | collective-permute-start | bytes 2752520 | tf_op jit(solution)/shard_map/ppermute | solution.py:135
  393.7 137.2 %collective-permute-start.73 = (bf16[3584,512]{1,0:T(8,128)(2,1)}, bf16[3584,512]{1,0:T(8,128)(2,1)}, u32[]{:S(2)}, u32[]{:S(2)}) collective-permute-start(bf16[3584,512]{1,0:T(8,128)(2,1)} %convolution_convert_fusion.1), channel_id=1, source_target_pairs={{0,1},{1,0},{2,3},{3,2},{4,5},{5,4},{6,7},{7,6},{8,9},{9,8},{10,11... | collective-permute-start | bytes 11010056 | tf_op jit(solution)/shard_map/ppermute | solution.py:261
  394.9 145.4 %collective-permute-start.74 = (bf16[512,3584]{1,0:T(8,128)(2,1)}, bf16[512,3584]{1,0:T(8,128)(2,1)S(1)}, u32[]{:S(2)}, u32[]{:S(2)}) collective-permute-start(bf16[512,3584]{1,0:T(8,128)(2,1)} %convolution_convert_fusion), channel_id=1, source_target_pairs={{0,1},{1,0},{2,3},{3,2},{4,5},{5,4},{6,7},{7,6},{8,9},{9,8},{10,11... | collective-permute-start | bytes 11010056 | tf_op jit(solution)/shard_map/ppermute | solution.py:260
  409.6 40.9 %collective-permute-start.51 = (bf16[64,3584]{1,0:T(8,128)(2,1)S(1)}, bf16[64,3584]{1,0:T(8,128)(2,1)S(1)}, u32[]{:S(2)}, u32[]{:S(2)}) collective-permute-start(bf16[64,3584]{1,0:T(8,128)(2,1)S(1)} %fusion.102), channel_id=1, source_target_pairs={{0,4},{2,6},{4,0},{6,2},{8,12},{10,14},{12,8},{14,10},{16,20},{18,... | collective-permute-start | bytes 1376264 | tf_op jit(solution)/shard_map/ppermute | solution.py:135
  448.3 19.7 %collective-permute-start.55 = (bf16[64,3584]{1,0:T(8,128)(2,1)S(1)}, bf16[64,3584]{1,0:T(8,128)(2,1)S(1)}, u32[]{:S(2)}, u32[]{:S(2)}) collective-permute-start(bf16[64,3584]{1,0:T(8,128)(2,1)S(1)} %add_convert_fusion.7), channel_id=1, source_target_pairs={{24,16},{26,18},{28,20},{30,22},{25,17},{27,19},{29,21},{31,23}} | collective-permute-start | bytes 1376264 | tf_op jit(solution)/shard_map/ppermute | solution.py:139
  449.6 19.7 %collective-permute-start.52 = (bf16[64,3584]{1,0:T(8,128)(2,1)S(1)}, bf16[64,3584]{1,0:T(8,128)(2,1)S(1)}, u32[]{:S(2)}, u32[]{:S(2)}) collective-permute-start(bf16[64,3584]{1,0:T(8,128)(2,1)S(1)} %add_convert_fusion.7), channel_id=1, source_target_pairs={{0,8},{2,10},{4,12},{6,14},{1,9},{3,11},{5,13},{7,15}} | collective-permute-start | bytes 1376264 | tf_op jit(solution)/shard_map/ppermute | solution.py:139
  450.5 20.9 %collective-permute-start.23 = (bf16[64,3584]{1,0:T(8,128)(2,1)S(1)}, bf16[64,3584]{1,0:T(8,128)(2,1)S(1)}, u32[]{:S(2)}, u32[]{:S(2)}) collective-permute-start(bf16[64,3584]{1,0:T(8,128)(2,1)S(1)} %fusion.110), channel_id=1, source_target_pairs={{0,2},{2,0},{4,6},{6,4},{8,10},{10,8},{12,14},{14,12},{16,18},{18,... | collective-permute-start | bytes 1376264 | tf_op jit(solution)/shard_map/ppermute | solution.py:135
  (95 other events, 1250.0 us)
